TPU v7x, 256 devices: a whole 4x4x8 slice. The times are simulated.
256 devices in a mesh: wide: 32 (over y, x, core), narrow: 8 (over z).
Axes of the slice: x: 4, y: 4, z: 8, core: 2. Of those that a mesh axis runs over, the one named last changes fastest.
Arguments:
- three_centre: bfloat16 [32, 1024, 4096], P('narrow', 'wide'), may hold values from -6 to 6
- go_blocks: bfloat16 [64, 64, 64], replicated, may hold values from -0.75 to 0.75
- gv_blocks: bfloat16 [64, 64, 64], replicated, may hold values from -0.125 to 0.125
- go_index: int32 [32, 32], P('narrow'), may hold values from 0 to 63
- gv_index: int32 [32, 32], P('narrow'), may hold values from 0 to 63
- source_mask: int32 [32, 32], P('narrow'), may hold values 0 or 1
Outputs:
- chi: float32 [1024, 1024], P('wide', 'narrow')
All inputs are finite; a program needn't handle non-finite values. No bound on the sum of `source_mask` on one device may be relied on, other than what follows from the above.
Results may differ from a plain program's by a relative error of at most 0.004.
Values may be sent and summed in bfloat16 or wider, within the bound.
No kernel may reach another device: no remote copies, remote signals or barrier semaphores. Data moves between devices by JAX's collectives and lax.ppermute only.
A program may use at most 192 MiB of HBM per device.

v0:
```python
import jax
import jax.numpy as jnp
from jax import lax
from jax.sharding import PartitionSpec as P


def local(three_centre, go_blocks, gv_blocks, go_index, gv_index, source_mask):
    local_pairs, aux_local, pair_width = three_centre.shape
    block = go_blocks.shape[1]
    go_chosen = go_blocks[go_index]
    gv_chosen = gv_blocks[gv_index] * source_mask.astype(jnp.bfloat16)[:, :, None, None]
    piece = lax.all_gather(three_centre, "narrow", axis=0, tiled=True)
    number_sources = piece.shape[0]
    sources = piece.reshape(number_sources, aux_local, block, block)
    results = []
    for target in range(local_pairs):
        first_product = jnp.einsum(
            "cma,cpmn->cpan", go_chosen[target], sources, preferred_element_type=jnp.float32
        ).astype(jnp.bfloat16)
        results.append(
            jnp.einsum(
                "cpan,cnd->pad",
                first_product,
                gv_chosen[target],
                preferred_element_type=jnp.float32,
            )
        )
    summed = jnp.stack(results)
    image = summed.reshape(local_pairs, aux_local, pair_width).astype(jnp.bfloat16)
    norm_scale = 1.0 / jnp.sqrt(jnp.float32(local_pairs * lax.axis_size("narrow") * pair_width))
    partial_chi = jnp.einsum(
        "kpe,kqe->pq",
        image,
        lax.all_gather(three_centre, "wide", axis=1, tiled=True),
        preferred_element_type=jnp.float32,
    )
    result = lax.psum_scatter(partial_chi, "narrow", scatter_dimension=1, tiled=True)
    return result * norm_scale


def solution(mesh):
    placed = (
        P("narrow", "wide", None),
        P(),
        P(),
        P("narrow", None),
        P("narrow", None),
        P("narrow", None),
    )
    return jax.shard_map(
        local, mesh=mesh, in_specs=placed, out_specs=P("wide", "narrow"), check_vma=False
    )
```

profile of v0, /device:TPU:12, one launch (start us, length us, event | category | flops | bytes accessed | tf_op | source)
XLA Modules:
  0.0 286.2 jit_solution(9310431331818708807)
XLA Ops:
  6.5 0.0 copy-start
  6.5 0.0 all-gather.3.cloned.1.call-start
  6.5 0.7 all-gather.3.cloned.1.call-update
  7.3 0.0 all-gather.5.cloned.1.call-start
  7.3 0.7 all-gather.5.cloned.1.call-update
  8.0 0.0 reduce-scatter.2.cloned.1.call-start
  8.1 0.7 compare_select_fusion
  8.7 0.1 reshape.28
  8.8 0.7 convert_element_type.30
  9.5 0.7 compare_select_fusion.1
  10.2 0.1 reshape.20
  10.3 0.0 copy-done
  10.3 1.0 gather_fusion.1
  11.3 3.4 %gather_fusion = bf16[128,64,64]{2,1,0:T(8,128)(2,1)} fusion(bf16[64,64,64]{2,1,0:T(8,128)(2,1)} %param.7, s32[1024]{0:T(1024)S(1)} %pad_clamp_fusion.1), kind=kCustom, calls=%fused_computation | custom fusion | bytes 2097664 | tf_op jit(solution)/shard_map/gather | solution.py:10
  14.7 1.5 broadcast_multiply_fusion
  16.2 90.0 %all-gather.3.cloned.1.call-done = bf16[32,32,4096]{2,1,0:T(8,128)(2,1)} async-done(((bf16[4,32,4096]{2,1,0:T(8,128)(2,1)}), bf16[32,32,4096]{2,1,0:T(8,128)(2,1)}) %all-gather.3.cloned.1.call-update) | async-done | bytes 8388624 | tf_op jit(solution)/shard_map/all_gather | solution.py:12
  106.2 23.6 %reshape.17 = bf16[32,32,64,64]{3,2,1,0:T(8,128)(2,1)} reshape(bf16[32,32,4096]{2,1,0:T(8,128)(2,1)} %all-gather.3.cloned.1.call-done) | data formatting | bytes 16777216 | tf_op jit(solution)/shard_map/reshape | solution.py:14
  129.8 0.0 copy-done.2
  129.8 10.7 %fusion.63 = bf16[32,64,64]{2,1,0:T(8,128)(2,1)S(1)} fusion(bf16[32,32,64,64]{3,2,1,0:T(8,128)(2,1)} %reshape.17, bf16[4,32,64,64]{3,2,1,0:T(8,128)(2,1)S(1)} %copy-done.2, bf16[128,64,64]{2,1,0:T(8,128)(2,1)} %gather_fusion), kind=kOutput, calls=%fused_computation.29 | convolution fusion | flops 1078067200 | bytes 18087936 | tf_op jit(solution)/shard_map/cpan,cnd->pad/dot_general | solution.py:21
  140.6 0.5 stack.15
  141.0 10.6 %fusion.58 = bf16[32,64,64]{2,1,0:T(8,128)(2,1)S(1)} fusion(bf16[32,32,64,64]{3,2,1,0:T(8,128)(2,1)} %reshape.17, bf16[4,32,64,64]{3,2,1,0:T(8,128)(2,1)S(1)} %copy-done.2, bf16[128,64,64]{2,1,0:T(8,128)(2,1)} %gather_fusion), kind=kOutput, calls=%fused_computation.28 | convolution fusion | flops 1078067200 | bytes 18087936 | tf_op jit(solution)/shard_map/cpan,cnd->pad/dot_general | solution.py:21
  151.6 1.2 stack.16
  152.8 12.7 %fusion.53 = bf16[32,64,64]{2,1,0:T(8,128)(2,1)S(1)} fusion(bf16[32,32,64,64]{3,2,1,0:T(8,128)(2,1)} %reshape.17, bf16[4,32,64,64]{3,2,1,0:T(8,128)(2,1)S(1)} %copy-done.2, bf16[128,64,64]{2,1,0:T(8,128)(2,1)} %gather_fusion), kind=kOutput, calls=%fused_computation.27 | convolution fusion | flops 1078067200 | bytes 18087936 | tf_op jit(solution)/shard_map/cpan,cnd->pad/dot_general | solution.py:21
  165.5 1.2 stack.17
  166.7 11.7 %fusion.48 = bf16[32,64,64]{2,1,0:T(8,128)(2,1)} fusion(bf16[32,32,64,64]{3,2,1,0:T(8,128)(2,1)} %reshape.17, bf16[4,32,64,64]{3,2,1,0:T(8,128)(2,1)S(1)} %copy-done.2, bf16[128,64,64]{2,1,0:T(8,128)(2,1)} %gather_fusion), kind=kOutput, calls=%fused_computation.26 | convolution fusion | flops 1078067200 | bytes 18087936 | tf_op jit(solution)/shard_map/cpan,cnd->pad/dot_general | solution.py:21
  178.4 1.6 stack.18
  180.0 44.6 %all-gather.5.cloned.1.call-done = bf16[4,1024,4096]{2,1,0:T(8,128)(2,1)} async-done(((bf16[4,32,4096]{2,1,0:T(8,128)(2,1)}), bf16[4,1024,4096]{2,1,0:T(8,128)(2,1)}) %all-gather.5.cloned.1.call-update) | async-done | bytes 33554448 | tf_op jit(solution)/shard_map/all_gather | solution.py:34
  224.6 16.0 %convolution_bitcast_fusion = f32[32,1024]{1,0:T(8,128)} fusion(bf16[4,1024,4096]{2,1,0:T(8,128)(2,1)} %all-gather.5.cloned.1.call-done, bf16[1,32,4096]{2,1,0:T(8,128)(2,1)S(1)} %stack.18, bf16[1,32,4096]{2,1,0:T(8,128)(2,1)} %stack.17, bf16[1,32,4096]{2,1,0:T(8,128)(2,1)} %stack.16, bf16[1,32,4096]{2,1,0:T(8,128)(2,1)S(1)} %stack.15), kind=kOutput, calls=%fused_computation.30 | convolution fusion | flops 1075314688 | bytes 34734080 | tf_op jit(solution)/shard_map/kpe,kqe->pq/dot_general | solution.py:31
  240.6 0.0 reduce-scatter.2.cloned.1.call-update
  240.6 37.7 %reduce-scatter.2.cloned.1.call-done = f32[32,128]{1,0:T(8,128)} async-done(((f32[32,1024]{1,0:T(8,128)}), f32[32,128]{1,0:T(8,128)}) %reduce-scatter.2.cloned.1.call-update) | async-done | bytes 16400 | tf_op jit(solution)/shard_map/reduce_scatter | solution.py:37
  278.4 1.3 broadcast_multiply_fusion.1
  279.7 0.0 copy-done.1
  (4 shorter events, 0.0 us)
Async XLA Ops:
  6.5 3.8 %copy-start = (bf16[64,64,64]{2,1,0:T(8,128)(2,1)S(1)}, bf16[64,64,64]{2,1,0:T(8,128)(2,1)}, u32[]{:S(2)}) copy-start(bf16[64,64,64]{2,1,0:T(8,128)(2,1)} %param.8) | copy-start | bytes 1572868
  6.5 99.6 %all-gather.3.cloned.1.call-start = ((), (), s32[]{:S(2)}) async-start(), calls=%async_computation.1 | async-start | bytes 9437184 | tf_op jit(solution)/shard_map/all_gather | solution.py:12
  7.3 217.3 %all-gather.5.cloned.1.call-start = ((), (), s32[]{:S(2)}) async-start(), calls=%async_computation.2 | async-start | bytes 34603008 | tf_op jit(solution)/shard_map/all_gather | solution.py:34
  8.0 270.4 %reduce-scatter.2.cloned.1.call-start = ((), (), s32[]{:S(2)}) async-start(), calls=%async_computation.3 | async-start | bytes 147456 | tf_op jit(solution)/shard_map/reduce_scatter | solution.py:37
  16.2 113.6 %copy-start.2 = (bf16[4,32,64,64]{3,2,1,0:T(8,128)(2,1)S(1)}, bf16[4,32,64,64]{3,2,1,0:T(8,128)(2,1)}, u32[]{:S(2)}) copy-start(bf16[4,32,64,64]{3,2,1,0:T(8,128)(2,1)} %broadcast_multiply_fusion) | copy-start | bytes 3145732
  178.4 101.3 %copy-start.1 = (bf16[64,64,64]{2,1,0:T(8,128)(2,1)S(1)}, bf16[64,64,64]{2,1,0:T(8,128)(2,1)}, u32[]{:S(2)}) copy-start(bf16[64,64,64]{2,1,0:T(8,128)(2,1)} %param.8) | copy-start | bytes 1572868
Sparse Core Ops, SparseCore 0:
  9.1 96.9 all-gather.2
  108.8 115.7 all-gather.4
  240.7 37.5 reduce-scatter.1
where the time goes:
time: 287 us; the launch traced here: 286 us
  waiting for transfers between devices  174 us (61%)
  matrix products  61.8 us (22%)
  local copies, waits for them, and re-layouts  32.6 us (11%)
  between operations  13.2 us (5%)
  other arithmetic  4.92 us (2%)
    all_gather x1, waiting for transfers between devices, local(): piece = lax.all_gather(three_centre, 'narrow', axis=0, tiled=True)  90 us
    dot_general x4, matrix products, local(): jnp.einsum('cpan,cnd->pad', first_product, gv_chosen[target], preferred_e...  45.7 us
    all_gather x1, waiting for transfers between devices, local(): lax.all_gather(three_centre, 'wide', axis=1, tiled=True)  44.6 us
    reduce_scatter x1, waiting for transfers between devices, local(): lax.psum_scatter(partial_chi, 'narrow', scatter_dimension=1, tiled=True)  37.7 us
    reshape x1, local copies, waits for them, and re-layouts, local(): sources = piece.reshape(number_sources, aux_local, block, block)  23.6 us
    dot_general x1, matrix products, local(): jnp.einsum('kpe,kqe->pq', image, lax.all_gather(three_centre, 'wide', axi...  16 us
  transfers between devices with their start and end apart: 3, of which 3 were waited for; matrix products, arithmetic and copies ran while one was open for 29% of the time, Pallas kernels for 0%

commit v1 on v0

--- a/solution.py
+++ b/solution.py
@@ -2,6 +2,13 @@
 import jax.numpy as jnp
 from jax import lax
 from jax.sharding import PartitionSpec as P
+
+
+def numbers_keep_up(content, dim_k):
+    raw_out = list(content.shape[1:])
+    raw_out[dim_k] *= content.shape[0]
+    latest = jnp.moveaxis(content, 0, dim_k).reshape(raw_out)
+    return latest
 
 
 def local(three_centre, go_blocks, gv_blocks, go_index, gv_index, source_mask):
@@ -9,7 +16,36 @@
     block = go_blocks.shape[1]
     go_chosen = go_blocks[go_index]
     gv_chosen = gv_blocks[gv_index] * source_mask.astype(jnp.bfloat16)[:, :, None, None]
-    piece = lax.all_gather(three_centre, "narrow", axis=0, tiled=True)
+
+    def quotas_resolve(page, mesh_name, join_dim):
+        amount_of = lax.axis_size(mesh_name)
+        buffers = []
+        nth = 0
+        while nth < amount_of:
+            buffers.append((nth, (nth + 1) % amount_of))
+            nth = nth + 1
+        lanes = []
+        for src_i, no in buffers:
+            lanes.append((no, src_i))
+        o_now, state_next = ([], [])
+        c = 0
+        while c < amount_of - 1:
+            if c % 2 == 0:
+                p_next = lax.ppermute(o_now[-1] if o_now else page, mesh_name, buffers)
+                o_now.append(p_next)
+            else:
+                state_next.append(
+                    lax.ppermute(state_next[-1] if state_next else page, mesh_name, lanes)
+                )
+            c += 1
+        work_now = jnp.stack([*o_now[::-1], page, *state_next])
+        carry_in = lax.axis_index(mesh_name)
+        f_next = carry_in - len(o_now)
+        work_now = work_now[(jnp.arange(amount_of) - f_next) % amount_of]
+        x_new = numbers_keep_up(work_now, join_dim)
+        return x_new
+
+    piece = quotas_resolve(three_centre, mesh_name="narrow", join_dim=0)
     number_sources = piece.shape[0]
     sources = piece.reshape(number_sources, aux_local, block, block)
     results = []

time: 287 us -> 266 us (0.927)
  waiting for transfers between devices: 174 us -> 120 us
  local copies, waits for them, and re-layouts: 32.6 us -> 55.5 us
  starting transfers between devices: 0.08 us -> 11.7 us
  matrix products: 61.8 us -> 58.4 us
    all_gather x1 -> x0, waiting for transfers between devices: 90 us -> none  [local(): piece = lax.all_gather(three_centre, 'narrow', axis=0, tiled=True)]
    ppermute x0 -> x7, waiting for transfers between devices: none -> 83.6 us  [the longest x4 83.6 us: quotas_resolve(): p_next = lax.ppermute(o_now[-1] if o_now else page, mesh_name, buffers)]
    all_gather x1, waiting for transfers between devices: 44.6 us -> 0.02 us  [local(): lax.all_gather(three_centre, 'wide', axis=1, tiled=True)]
    another operation x0 -> x2, local copies, waits for them, and re-layouts: none -> 24.9 us  [the longest x1 23.8 us: local(): sources = piece.reshape(number_sources, aux_local, block, block)]
    reshape x1 -> x0, local copies, waits for them, and re-layouts: 23.6 us -> none  [local(): sources = piece.reshape(number_sources, aux_local, block, block)]
    unnamed x6 -> x23, local copies, waits for them, and re-layouts: 0.01 us -> 14.4 us
    ppermute x0 -> x7, starting transfers between devices: none -> 11.7 us  [the longest x3 9.69 us: quotas_resolve(): lax.ppermute(state_next[-1] if state_next else page, mesh_name, lanes)]
    gather x0 -> x1, local copies, waits for them, and re-layouts: none -> 8.41 us  [quotas_resolve(): work_now = work_now[(jnp.arange(amount_of) - f_next) % amount_of]]
  transfers between devices with their start and end apart: 3 -> 9, of which waited for: 3 -> 5; matrix products, arithmetic and copies ran while one was open for 29% -> 38% of each run, Pallas kernels for 0% -> 0%
where the time goes in v1:
time: 266 us; the launch traced here: 264 us
  waiting for transfers between devices  120 us (45%)
  matrix products  58.4 us (22%)
  local copies, waits for them, and re-layouts  55.5 us (21%)
  between operations  13.5 us (5%)
  starting transfers between devices  11.7 us (4%)
  other arithmetic  4.95 us (2%)
    ppermute x4, waiting for transfers between devices, quotas_resolve(): p_next = lax.ppermute(o_now[-1] if o_now else page, mesh_name, buffers)  83.6 us
    dot_general x4, matrix products, local(): jnp.einsum('cpan,cnd->pad', first_product, gv_chosen[target], preferred_e...  42.3 us
    reduce_scatter x1, waiting for transfers between devices, local(): lax.psum_scatter(partial_chi, 'narrow', scatter_dimension=1, tiled=True)  35.9 us
    another operation x1, local copies, waits for them, and re-layouts, local(): sources = piece.reshape(number_sources, aux_local, block, block)  23.8 us
    dot_general x1, matrix products, local(): jnp.einsum('kpe,kqe->pq', image, lax.all_gather(three_centre, 'wide', axi...  16.1 us
    unnamed x23, local copies, waits for them, and re-layouts  14.4 us
    ppermute x3, starting transfers between devices, quotas_resolve(): lax.ppermute(state_next[-1] if state_next else page, mesh_name, lanes)  9.69 us
    gather x1, local copies, waits for them, and re-layouts, quotas_resolve(): work_now = work_now[(jnp.arange(amount_of) - f_next) % amount_of]  8.41 us
  transfers between devices with their start and end apart: 9, of which 5 were waited for; matrix products, arithmetic and copies ran while one was open for 38% of the time, Pallas kernels for 0%

profile of v1, /device:TPU:12, one launch (start us, length us, event | category | flops | bytes accessed | tf_op | source)
XLA Modules:
  0.0 264.4 jit_solution(8585225187400435794)
XLA Ops:
  7.3 2.0 collective-permute-start
  9.3 27.3 %collective-permute-done = bf16[4,32,4096]{2,1,0:T(8,128)(2,1)S(1)} collective-permute-done((bf16[4,32,4096]{2,1,0:T(8,128)(2,1)}, bf16[4,32,4096]{2,1,0:T(8,128)(2,1)S(1)}, u32[]{:S(2)}, u32[]{:S(2)}) %collective-permute-start) | collective-permute-done | bytes 1048608 | tf_op jit(solution)/shard_map/ppermute | solution.py:34
  36.6 0.9 copy-done.4
  37.6 3.2 %collective-permute-start.4 = (bf16[4,32,4096]{2,1,0:T(8,128)(2,1)}, bf16[4,32,4096]{2,1,0:T(8,128)(2,1)}, u32[]{:S(2)}, u32[]{:S(2)}) collective-permute-start(bf16[4,32,4096]{2,1,0:T(8,128)(2,1)} %param.6), channel_id=1, source_target_pairs={{1,0},{2,1},{3,2},{4,3},{5,4},{6,5},{7,6},{0,7},{9,8},{10,9},{11,1... | collective-permute-start | bytes 3145736 | tf_op jit(solution)/shard_map/ppermute | solution.py:38
  40.8 22.3 %collective-permute-done.1 = bf16[4,32,4096]{2,1,0:T(8,128)(2,1)S(1)} collective-permute-done((bf16[4,32,4096]{2,1,0:T(8,128)(2,1)S(1)}, bf16[4,32,4096]{2,1,0:T(8,128)(2,1)S(1)}, u32[]{:S(2)}, u32[]{:S(2)}) %collective-permute-start.1) | collective-permute-done | bytes 1048608 | tf_op jit(solution)/shard_map/ppermute | solution.py:34
  63.1 1.0 copy-done.6
  64.1 3.2 %collective-permute-start.5 = (bf16[4,32,4096]{2,1,0:T(8,128)(2,1)}, bf16[4,32,4096]{2,1,0:T(8,128)(2,1)}, u32[]{:S(2)}, u32[]{:S(2)}) collective-permute-start(bf16[4,32,4096]{2,1,0:T(8,128)(2,1)} %collective-permute-done.4), channel_id=1, source_target_pairs={{1,0},{2,1},{3,2},{4,3},{5,4},{6,5},{7,6},{0,7},{9,8},{10,9},{11,1... | collective-permute-start | bytes 3145736 | tf_op jit(solution)/shard_map/ppermute | solution.py:38
  67.3 21.5 %collective-permute-done.2 = bf16[4,32,4096]{2,1,0:T(8,128)(2,1)} collective-permute-done((bf16[4,32,4096]{2,1,0:T(8,128)(2,1)S(1)}, bf16[4,32,4096]{2,1,0:T(8,128)(2,1)}, u32[]{:S(2)}, u32[]{:S(2)}) %collective-permute-start.2) | collective-permute-done | bytes 1048608 | tf_op jit(solution)/shard_map/ppermute | solution.py:34
  91.1 1.0 gather_fusion.2
  92.1 3.5 %gather_fusion.1 = bf16[128,64,64]{2,1,0:T(8,128)(2,1)} fusion(bf16[64,64,64]{2,1,0:T(8,128)(2,1)} %param.7, s32[1024]{0:T(1024)S(1)} %pad_clamp_fusion.1), kind=kCustom, calls=%fused_computation.1 | custom fusion | bytes 2097664 | tf_op jit(solution)/shard_map/gather | solution.py:17
  95.6 1.5 broadcast_multiply_fusion
  97.1 3.2 %collective-permute-start.6 = (bf16[4,32,4096]{2,1,0:T(8,128)(2,1)}, bf16[4,32,4096]{2,1,0:T(8,128)(2,1)S(1)}, u32[]{:S(2)}, u32[]{:S(2)}) collective-permute-start(bf16[4,32,4096]{2,1,0:T(8,128)(2,1)} %collective-permute-done.5), channel_id=1, source_target_pairs={{1,0},{2,1},{3,2},{4,3},{5,4},{6,5},{7,6},{0,7},{9,8},{10,9},{11,1... | collective-permute-start | bytes 3145736 | tf_op jit(solution)/shard_map/ppermute | solution.py:38
  100.3 12.5 %collective-permute-done.3 = bf16[4,32,4096]{2,1,0:T(8,128)(2,1)} collective-permute-done((bf16[4,32,4096]{2,1,0:T(8,128)(2,1)}, bf16[4,32,4096]{2,1,0:T(8,128)(2,1)}, u32[]{:S(2)}, u32[]{:S(2)}) %collective-permute-start.3) | collective-permute-done | bytes 1048608 | tf_op jit(solution)/shard_map/ppermute | solution.py:34
  112.8 2.3 bitcast_dynamic-update-slice_fusion.7
  115.2 2.3 bitcast_dynamic-update-slice_fusion.6
  117.5 1.0 bitcast_dynamic-update-slice_fusion.5
  118.5 1.1 bitcast_dynamic-update-slice_fusion.4
  119.6 1.1 bitcast_dynamic-update-slice_fusion.3
  120.7 2.3 bitcast_dynamic-update-slice_fusion.2
  123.0 2.3 bitcast_dynamic-update-slice_fusion.1
  125.3 1.1 bitcast_dynamic-update-slice_fusion
  126.4 8.4 %gather_fusion = bf16[8,4,32,4096]{3,2,1,0:T(8,128)(2,1)} fusion(bf16[8,4,32,4096]{3,2,1,0:T(8,128)(2,1)} %bitcast_dynamic-update-slice_fusion, s32[1024]{0:T(1024)S(1)} %pad_clamp_fusion.2), kind=kCustom, calls=%fused_computation | custom fusion | bytes 16777248 | tf_op jit(solution)/shard_map/gather | solution.py:44
  134.8 23.8 %reshape_reshape.3 = bf16[32,32,64,64]{3,2,1,0:T(8,128)(2,1)} reshape(bf16[8,4,32,4096]{3,2,1,0:T(8,128)(2,1)} %gather_fusion) | data formatting | bytes 16777216 | tf_op jit(solution)/shard_map/reshape;reshape | solution.py:50
  158.6 10.6 %fusion.63 = bf16[32,64,64]{2,1,0:T(8,128)(2,1)S(1)} fusion(bf16[32,32,64,64]{3,2,1,0:T(8,128)(2,1)} %reshape_reshape.3, bf16[4,32,64,64]{3,2,1,0:T(8,128)(2,1)S(1)} %copy-done.3, bf16[128,64,64]{2,1,0:T(8,128)(2,1)} %gather_fusion.1), kind=kOutput, calls=%fused_computation.30 | convolution fusion | flops 1078067200 | bytes 18087936 | tf_op jit(solution)/shard_map/cpan,cnd->pad/dot_general | solution.py:57
  169.6 10.6 %fusion.58 = bf16[32,64,64]{2,1,0:T(8,128)(2,1)S(1)} fusion(bf16[32,32,64,64]{3,2,1,0:T(8,128)(2,1)} %reshape_reshape.3, bf16[4,32,64,64]{3,2,1,0:T(8,128)(2,1)S(1)} %copy-done.3, bf16[128,64,64]{2,1,0:T(8,128)(2,1)} %gather_fusion.1), kind=kOutput, calls=%fused_computation.29 | convolution fusion | flops 1078067200 | bytes 18087936 | tf_op jit(solution)/shard_map/cpan,cnd->pad/dot_general | solution.py:57
  180.2 1.2 stack.52
  181.4 10.6 %fusion.53 = bf16[32,64,64]{2,1,0:T(8,128)(2,1)S(1)} fusion(bf16[32,32,64,64]{3,2,1,0:T(8,128)(2,1)} %reshape_reshape.3, bf16[4,32,64,64]{3,2,1,0:T(8,128)(2,1)S(1)} %copy-done.3, bf16[128,64,64]{2,1,0:T(8,128)(2,1)} %gather_fusion.1), kind=kOutput, calls=%fused_computation.28 | convolution fusion | flops 1078067200 | bytes 18087936 | tf_op jit(solution)/shard_map/cpan,cnd->pad/dot_general | solution.py:57
  192.0 1.2 stack.53
  193.1 10.6 %fusion.48 = bf16[32,64,64]{2,1,0:T(8,128)(2,1)S(1)} fusion(bf16[32,32,64,64]{3,2,1,0:T(8,128)(2,1)} %reshape_reshape.3, bf16[4,32,64,64]{3,2,1,0:T(8,128)(2,1)S(1)} %copy-done.3, bf16[128,64,64]{2,1,0:T(8,128)(2,1)} %gather_fusion.1), kind=kOutput, calls=%fused_computation.27 | convolution fusion | flops 1078067200 | bytes 18087936 | tf_op jit(solution)/shard_map/cpan,cnd->pad/dot_general | solution.py:57
  204.2 16.1 %convolution_bitcast_fusion = f32[32,1024]{1,0:T(8,128)} fusion(bf16[4,1024,4096]{2,1,0:T(8,128)(2,1)} %all-gather.2.cloned.1.call-done, bf16[1,32,4096]{2,1,0:T(8,128)(2,1)S(1)} %stack.54, bf16[1,32,4096]{2,1,0:T(8,128)(2,1)} %stack.53, bf16[1,32,4096]{2,1,0:T(8,128)(2,1)} %stack.52, bf16[1,32,4096]{2,1,0:T(8,128)(2,1)S(1)} %stack.51), kind=kOutput, calls=%fused_computation.31 | convolution fusion | flops 1075314688 | bytes 34734080 | tf_op jit(solution)/shard_map/kpe,kqe->pq/dot_general | solution.py:67
  220.3 35.9 %reduce-scatter.2.cloned.1.call-done = f32[32,128]{1,0:T(8,128)} async-done(((f32[32,1024]{1,0:T(8,128)}), f32[32,128]{1,0:T(8,128)}) %reduce-scatter.2.cloned.1.call-update) | async-done | bytes 16400 | tf_op jit(solution)/shard_map/reduce_scatter | solution.py:73
  256.3 1.3 broadcast_multiply_fusion.1
  (36 shorter events, 4.0 us)
Async XLA Ops:
  6.5 84.5 %copy-start = (bf16[64,64,64]{2,1,0:T(8,128)(2,1)S(1)}, bf16[64,64,64]{2,1,0:T(8,128)(2,1)}, u32[]{:S(2)}) copy-start(bf16[64,64,64]{2,1,0:T(8,128)(2,1)} %param.8) | copy-start | bytes 1572868
  6.5 197.7 %all-gather.2.cloned.1.call-start = ((), (), s32[]{:S(2)}) async-start(), calls=%async_computation.1 | async-start | bytes 34603008 | tf_op jit(solution)/shard_map/all_gather | solution.py:70
  7.3 249.0 %reduce-scatter.2.cloned.1.call-start = ((), (), s32[]{:S(2)}) async-start(), calls=%async_computation.2 | async-start | bytes 147456 | tf_op jit(solution)/shard_map/reduce_scatter | solution.py:73
  7.3 29.3 %collective-permute-start = (bf16[4,32,4096]{2,1,0:T(8,128)(2,1)}, bf16[4,32,4096]{2,1,0:T(8,128)(2,1)S(1)}, u32[]{:S(2)}, u32[]{:S(2)}) collective-permute-start(bf16[4,32,4096]{2,1,0:T(8,128)(2,1)} %param.6), channel_id=1, source_target_pairs={{0,1},{1,2},{2,3},{3,4},{4,5},{5,6},{6,7},{7,0},{8,9},{9,10},{10,1... | collective-permute-start | bytes 3145736 | tf_op jit(solution)/shard_map/ppermute | solution.py:34
  36.6 0.9 copy-start.4
  37.6 25.6 %collective-permute-start.1 = (bf16[4,32,4096]{2,1,0:T(8,128)(2,1)S(1)}, bf16[4,32,4096]{2,1,0:T(8,128)(2,1)S(1)}, u32[]{:S(2)}, u32[]{:S(2)}) collective-permute-start(bf16[4,32,4096]{2,1,0:T(8,128)(2,1)S(1)} %collective-permute-done), channel_id=1, source_target_pairs={{0,1},{1,2},{2,3},{3,4},{4,5},{5,6},{6,7},{7,0},{8,9},{9,10},{10,1... | collective-permute-start | bytes 3145736 | tf_op jit(solution)/shard_map/ppermute | solution.py:34
  37.6 26.5 %collective-permute-start.4 = (bf16[4,32,4096]{2,1,0:T(8,128)(2,1)}, bf16[4,32,4096]{2,1,0:T(8,128)(2,1)}, u32[]{:S(2)}, u32[]{:S(2)}) collective-permute-start(bf16[4,32,4096]{2,1,0:T(8,128)(2,1)} %param.6), channel_id=1, source_target_pairs={{1,0},{2,1},{3,2},{4,3},{5,4},{6,5},{7,6},{0,7},{9,8},{10,9},{11,1... | collective-permute-start | bytes 3145736 | tf_op jit(solution)/shard_map/ppermute | solution.py:38
  63.1 1.0 copy-start.6
  64.1 24.7 %collective-permute-start.2 = (bf16[4,32,4096]{2,1,0:T(8,128)(2,1)S(1)}, bf16[4,32,4096]{2,1,0:T(8,128)(2,1)}, u32[]{:S(2)}, u32[]{:S(2)}) collective-permute-start(bf16[4,32,4096]{2,1,0:T(8,128)(2,1)S(1)} %collective-permute-done.1), channel_id=1, source_target_pairs={{0,1},{1,2},{2,3},{3,4},{4,5},{5,6},{6,7},{7,0},{8,9},{9,10},{10,1... | collective-permute-start | bytes 3145736 | tf_op jit(solution)/shard_map/ppermute | solution.py:34
  64.1 33.0 %collective-permute-start.5 = (bf16[4,32,4096]{2,1,0:T(8,128)(2,1)}, bf16[4,32,4096]{2,1,0:T(8,128)(2,1)}, u32[]{:S(2)}, u32[]{:S(2)}) collective-permute-start(bf16[4,32,4096]{2,1,0:T(8,128)(2,1)} %collective-permute-done.4), channel_id=1, source_target_pairs={{1,0},{2,1},{3,2},{4,3},{5,4},{6,5},{7,6},{0,7},{9,8},{10,9},{11,1... | collective-permute-start | bytes 3145736 | tf_op jit(solution)/shard_map/ppermute | solution.py:38
  88.8 24.0 %collective-permute-start.3 = (bf16[4,32,4096]{2,1,0:T(8,128)(2,1)}, bf16[4,32,4096]{2,1,0:T(8,128)(2,1)}, u32[]{:S(2)}, u32[]{:S(2)}) collective-permute-start(bf16[4,32,4096]{2,1,0:T(8,128)(2,1)} %collective-permute-done.2), channel_id=1, source_target_pairs={{0,1},{1,2},{2,3},{3,4},{4,5},{5,6},{6,7},{7,0},{8,9},{9,10},{10,1... | collective-permute-start | bytes 3145736 | tf_op jit(solution)/shard_map/ppermute | solution.py:34
  92.1 27.6 %copy-start.2 = (bf16[4,32,4096]{2,1,0:T(8,128)(2,1)S(1)}, bf16[4,32,4096]{2,1,0:T(8,128)(2,1)}, u32[]{:S(2)}) copy-start(bf16[4,32,4096]{2,1,0:T(8,128)(2,1)} %param.6) | copy-start | bytes 3145732
  95.6 21.9 %copy-start.7 = (bf16[4,32,4096]{2,1,0:T(8,128)(2,1)S(1)}, bf16[4,32,4096]{2,1,0:T(8,128)(2,1)}, u32[]{:S(2)}) copy-start(bf16[4,32,4096]{2,1,0:T(8,128)(2,1)} %copy-done.6) | copy-start | bytes 3145732
  95.6 22.9 %copy-start.5 = (bf16[4,32,4096]{2,1,0:T(8,128)(2,1)S(1)}, bf16[4,32,4096]{2,1,0:T(8,128)(2,1)}, u32[]{:S(2)}) copy-start(bf16[4,32,4096]{2,1,0:T(8,128)(2,1)} %copy-done.4) | copy-start | bytes 3145732
  97.1 28.2 %collective-permute-start.6 = (bf16[4,32,4096]{2,1,0:T(8,128)(2,1)}, bf16[4,32,4096]{2,1,0:T(8,128)(2,1)S(1)}, u32[]{:S(2)}, u32[]{:S(2)}) collective-permute-start(bf16[4,32,4096]{2,1,0:T(8,128)(2,1)} %collective-permute-done.5), channel_id=1, source_target_pairs={{1,0},{2,1},{3,2},{4,3},{5,4},{6,5},{7,6},{0,7},{9,8},{10,9},{11,1... | collective-permute-start | bytes 3145736 | tf_op jit(solution)/shard_map/ppermute | solution.py:38
  134.8 23.8 %copy-start.3 = (bf16[4,32,64,64]{3,2,1,0:T(8,128)(2,1)S(1)}, bf16[4,32,64,64]{3,2,1,0:T(8,128)(2,1)}, u32[]{:S(2)}) copy-start(bf16[4,32,64,64]{3,2,1,0:T(8,128)(2,1)} %broadcast_multiply_fusion) | copy-start | bytes 3145732
  204.2 53.4 %copy-start.1 = (bf16[64,64,64]{2,1,0:T(8,128)(2,1)S(1)}, bf16[64,64,64]{2,1,0:T(8,128)(2,1)}, u32[]{:S(2)}) copy-start(bf16[64,64,64]{2,1,0:T(8,128)(2,1)} %param.8) | copy-start | bytes 1572868
Sparse Core Ops, SparseCore 0:
  10.0 120.0 all-gather.1
  220.5 35.7 reduce-scatter.1
